TPU v7x, 32 devices: a whole 2x2x4 slice. The times are simulated.
32 devices in a mesh: dp: 8 (over y, x, core), tensor: 4 (over z).
Axes of the slice: x: 2, y: 2, z: 4, core: 2. Of those that a mesh axis runs over, the one named last changes fastest.
Arguments:
- block_in: float32 [4096, 1024], P(('dp', 'tensor')), may hold values from -6 to 6
- cotangent: float32 [4096, 1024], P(('dp', 'tensor')), may hold values from -6 to 6
- routes: int32 [4096, 8], P('dp'), may hold values from 0 to 15, all different within a row; in each aligned block of 512 rows (0 to 511, 512 to 1023, ...) at most 288 rows name the same one
- gate_weights: float32 [4096, 8], P('dp'), may hold values from 0.02 to 0.3
- norm_gains: float32 [2, 1024], P(None, 'dp'), may hold values from 0.5 to 1.5
- attention_weight: float32 [4, 1024, 512], P(None, 'dp', 'tensor'), may hold values from -0.1875 to 0.1875
- output_weight: float32 [2, 1024, 512], P(None, 'dp', 'tensor'), may hold values from -0.75 to 0.75
- w_gate_up: float32 [16, 2, 1024, 512], P(None, None, 'dp', 'tensor'), may hold values from -0.1875 to 0.1875
- w_down: float32 [16, 1024, 512], P(None, 'dp', 'tensor'), may hold values from -0.75 to 0.75
- m_gains: float32 [2, 1024], P(None, 'dp'), may hold values from -128 to 128
- v_gains: float32 [2, 1024], P(None, 'dp'), may hold values from 100 to 10000
- attention_first_moment: float32 [4, 1024, 512], P(None, 'dp', 'tensor'), may hold values from -12 to 12
- attention_second_moment: float32 [4, 1024, 512], P(None, 'dp', 'tensor'), may hold values from 1 to 100
- output_first_moment: float32 [2, 1024, 512], P(None, 'dp', 'tensor'), may hold values from -16 to 16
- output_second_moment: float32 [2, 1024, 512], P(None, 'dp', 'tensor'), may hold values from 1 to 100
- m_gate_up: float32 [16, 2, 1024, 512], P(None, None, 'dp', 'tensor'), may hold values from -32 to 32
- v_gate_up: float32 [16, 2, 1024, 512], P(None, None, 'dp', 'tensor'), may hold values from 10 to 1000
- m_down: float32 [16, 1024, 512], P(None, 'dp', 'tensor'), may hold values from -12 to 12
- v_down: float32 [16, 1024, 512], P(None, 'dp', 'tensor'), may hold values from 1 to 100
Outputs:
- block_out: float32 [4096, 1024], P(('dp', 'tensor'))
- input_grad: float32 [4096, 1024], P(('dp', 'tensor'))
- grad_gains: float32 [2, 1024], P(None, 'dp')
- grad_attn: float32 [4, 1024, 512], P(None, 'dp', 'tensor')
- grad_out: float32 [2, 1024, 512], P(None, 'dp', 'tensor')
- grad_gate_up: float32 [16, 2, 1024, 512], P(None, None, 'dp', 'tensor')
- grad_down: float32 [16, 1024, 512], P(None, 'dp', 'tensor')
- new_gains: float32 [2, 1024], P(None, 'dp')
- new_attn: float32 [4, 1024, 512], P(None, 'dp', 'tensor')
- new_out: float32 [2, 1024, 512], P(None, 'dp', 'tensor')
- new_gate_up: float32 [16, 2, 1024, 512], P(None, None, 'dp', 'tensor')
- new_down: float32 [16, 1024, 512], P(None, 'dp', 'tensor')
- new_m_gains: float32 [2, 1024], P(None, 'dp')
- new_v_gains: float32 [2, 1024], P(None, 'dp')
- new_m_attn: float32 [4, 1024, 512], P(None, 'dp', 'tensor')
- new_v_attn: float32 [4, 1024, 512], P(None, 'dp', 'tensor')
- new_m_out: float32 [2, 1024, 512], P(None, 'dp', 'tensor')
- new_v_out: float32 [2, 1024, 512], P(None, 'dp', 'tensor')
- new_m_gate_up: float32 [16, 2, 1024, 512], P(None, None, 'dp', 'tensor')
- new_v_gate_up: float32 [16, 2, 1024, 512], P(None, None, 'dp', 'tensor')
- new_m_down: float32 [16, 1024, 512], P(None, 'dp', 'tensor')
- new_v_down: float32 [16, 1024, 512], P(None, 'dp', 'tensor')
Inputs may be any that keep to these rules, and one draw needn't show every extreme that they name: `routes`: each row names 8 different experts. Within each aligned block of 512 rows no expert is named by more than 288 rows, and in some block one expert is named by exactly 288 rows.
All inputs are finite; a program needn't handle non-finite values.
Results may differ from a plain program's by a relative error of at most 0.015.
The roundings to bfloat16 on the way count: a program that leaves them out, or rounds other values in their place, can miss the bound.
Values may be sent and summed in bfloat16 or wider, within the bound.
A program may use at most 192 MiB of HBM per device.

v0:
```python
import jax
import jax.numpy as jnp
from jax import lax
from jax.sharding import PartitionSpec as P

HEAD_SIZE = 64
E = 16
SEQ = 512
STEP = 3
CAP = 288
norm_eps = 1e-05
beta_one = 0.9
beta_two = 0.95
adam_eps = 1e-08
rate_matrix = 0.02
rate_gain = 0.2
decay_matrix = 0.1
rope_base = 10000.0


def rope_tables(length, width):
    half_width = width // 2
    frequency = rope_base ** (-(2.0 * jnp.arange(half_width, dtype=jnp.float32)) / width)
    angles = jnp.arange(length, dtype=jnp.float32)[:, None] * frequency[None, :]
    return (jnp.cos(angles)[:, None, :], jnp.sin(angles)[:, None, :])


def rotate(vectors, cos_table, sine_table):
    half_width = vectors.shape[-1] // 2
    lower_half = vectors[..., :half_width]
    upper_half = vectors[..., half_width:]
    return jnp.concatenate(
        [
            lower_half * cos_table - upper_half * sine_table,
            upper_half * cos_table + lower_half * sine_table,
        ],
        axis=-1,
    )


def unrotate(vectors, cos_table, sine_table):
    half_width = vectors.shape[-1] // 2
    lower_half = vectors[..., :half_width]
    upper_half = vectors[..., half_width:]
    return jnp.concatenate(
        [
            lower_half * cos_table + upper_half * sine_table,
            upper_half * cos_table - lower_half * sine_table,
        ],
        axis=-1,
    )


def causal_scores(queries, keys_rot):
    scale = queries.shape[-1] ** (-0.5)
    scores = (
        jnp.einsum("jqgh,kgh->jgqk", queries, keys_rot, preferred_element_type=jnp.float32) * scale
    )
    length = scores.shape[-1]
    allowed = lax.broadcasted_iota(jnp.int32, (length, length), 0) >= lax.broadcasted_iota(
        jnp.int32, (length, length), 1
    )
    return jnp.where(allowed, scores, -jnp.inf)


def attend(items):
    queries, keys_rot, values = items
    scores = causal_scores(queries, keys_rot)
    log_totals = jax.nn.logsumexp(scores, axis=-1)
    softmax_b = jnp.exp(scores - log_totals[..., None]).astype(jnp.bfloat16)
    attended = jnp.einsum(
        "jgqk,kgh->jqgh", softmax_b, values, preferred_element_type=jnp.float32
    ).astype(jnp.bfloat16)
    return (attended, log_totals)


def attend_back(items):
    queries, keys_rot, values, attended, log_totals, attended_cot = items
    scale = queries.shape[-1] ** (-0.5)
    scores = causal_scores(queries, keys_rot)
    softmax_f = jnp.exp(scores - log_totals[..., None])
    softmax_b = softmax_f.astype(jnp.bfloat16)
    value_cot = jnp.einsum(
        "jgqk,jqgh->kgh", softmax_b, attended_cot, preferred_element_type=jnp.float32
    )
    weight_cot = jnp.einsum(
        "jqgh,kgh->jgqk", attended_cot, values, preferred_element_type=jnp.float32
    )
    row_dots = jnp.einsum(
        "jqgh,jqgh->jgq", attended_cot, attended, preferred_element_type=jnp.float32
    )
    score_cot = (softmax_f * (weight_cot - row_dots[..., None])).astype(jnp.bfloat16)
    query_cot = (
        jnp.einsum("jgqk,kgh->jqgh", score_cot, keys_rot, preferred_element_type=jnp.float32)
        * scale
    )
    key_cot = (
        jnp.einsum("jgqk,jqgh->kgh", score_cot, queries, preferred_element_type=jnp.float32) * scale
    )
    return (query_cot, key_cot, value_cot)


def slot_table(route_rows, gate_rows, tok_count):
    hits = (route_rows[:, :, None] == jnp.arange(E, dtype=jnp.int32)[None, None, :]).astype(
        jnp.int32
    )
    per_token = jnp.sum(hits, axis=1, dtype=jnp.int32)
    before = jnp.cumsum(per_token, axis=0, dtype=jnp.int32) - per_token
    position = jnp.sum(hits * before[:, None, :], axis=2, dtype=jnp.int32)
    flat_slot = (route_rows * CAP + position).reshape(-1)
    owner = jnp.broadcast_to(
        jnp.arange(tok_count, dtype=jnp.int32)[:, None], route_rows.shape
    ).reshape(-1)
    slot_token = jnp.full((E * CAP,), tok_count, jnp.int32).at[flat_slot].set(owner)
    slot_weight = jnp.zeros((E * CAP,), jnp.float32).at[flat_slot].set(gate_rows.reshape(-1))
    return (slot_token, slot_weight)


def fetch_experts(w_gate_up, w_down, start_expert, per_turn):
    gate_up_part = w_gate_up[start_expert : start_expert + per_turn].astype(jnp.bfloat16)
    down_part = w_down[start_expert : start_expert + per_turn].astype(jnp.bfloat16)
    return (
        lax.all_gather(gate_up_part, "dp", axis=2, tiled=True),
        lax.all_gather(down_part, "dp", axis=1, tiled=True),
    )


def adamw_update(weight, moment_one, moment_two, gradient, rate, decay):
    new_one = beta_one * moment_one + (1.0 - beta_one) * gradient
    new_two = beta_two * moment_two + (1.0 - beta_two) * gradient * gradient
    corrected_one = new_one / (1.0 - beta_one**STEP)
    corrected_two = new_two / (1.0 - beta_two**STEP)
    new_weight = weight - rate * (
        corrected_one / (jnp.sqrt(corrected_two) + adam_eps) + decay * weight
    )
    return (new_weight, new_one, new_two)


def local(
    block_in,
    cotangent,
    routes,
    gate_weights,
    norm_gains,
    attention_weight,
    output_weight,
    w_gate_up,
    w_down,
    m_gains,
    v_gains,
    attention_first_moment,
    attention_second_moment,
    output_first_moment,
    output_second_moment,
    m_gate_up,
    v_gate_up,
    m_down,
    v_down,
):
    gains_all, attn_all, out_all = (
        lax.all_gather(norm_gains.astype(jnp.bfloat16), "dp", axis=1, tiled=True),
        lax.all_gather(attention_weight.astype(jnp.bfloat16), "dp", axis=1, tiled=True),
        lax.all_gather(output_weight.astype(jnp.bfloat16), "dp", axis=1, tiled=True),
    )
    tok_count = routes.shape[0]
    seq_count = tok_count // SEQ
    width = block_in.shape[1]
    kv_count = attn_all.shape[2] // HEAD_SIZE
    cos_table, sine_table = rope_tables(SEQ, HEAD_SIZE)
    gain_one = gains_all[0].astype(jnp.float32)
    gain_two = gains_all[1].astype(jnp.float32)
    inv_one = lax.rsqrt(jnp.mean(block_in * block_in, axis=1, keepdims=True) + norm_eps)
    normed_one = (block_in * inv_one * gain_one).astype(jnp.bfloat16)
    tokens_one = lax.all_gather(normed_one, "tensor", axis=0, tiled=True)
    projected = jnp.einsum("td,zdc->ztc", tokens_one, attn_all, preferred_element_type=jnp.float32)
    head_vals = projected.reshape(4, seq_count, SEQ, kv_count, HEAD_SIZE)
    queries = (
        rotate(head_vals[0:2], cos_table, sine_table).astype(jnp.bfloat16).transpose(1, 0, 2, 3, 4)
    )
    keys_rot = rotate(head_vals[2], cos_table, sine_table).astype(jnp.bfloat16)
    values = head_vals[3].astype(jnp.bfloat16)
    attended, log_totals = lax.map(attend, (queries, keys_rot, values))
    attended_flat = attended.transpose(1, 0, 2, 3, 4).reshape(2, tok_count, kv_count * HEAD_SIZE)
    partial_value = jnp.einsum(
        "jtc,jdc->td", attended_flat, out_all, preferred_element_type=jnp.float32
    )
    residual = block_in + lax.psum_scatter(partial_value, "tensor", scatter_dimension=0, tiled=True)
    inv_two = lax.rsqrt(jnp.mean(residual * residual, axis=1, keepdims=True) + norm_eps)
    normed_two = (residual * inv_two * gain_two).astype(jnp.bfloat16)
    tokens_two = lax.all_gather(normed_two, "tensor", axis=0, tiled=True)
    slot_token, slot_weight = slot_table(routes, gate_weights, tok_count)
    padded = jnp.concatenate([tokens_two, jnp.zeros((1, width), jnp.bfloat16)], axis=0)
    expert_in = padded[slot_token].reshape(E, CAP, width)
    per_turn = 8
    mixture = jnp.zeros((tok_count + 1, width), jnp.float32)
    saved_acts = []
    for start_expert in range(0, E, per_turn):
        gate_up_g, down_g = fetch_experts(w_gate_up, w_down, start_expert, per_turn)
        inputs = expert_in[start_expert : start_expert + per_turn]
        gate_up = jnp.einsum(
            "ecd,ezdf->zecf", inputs, gate_up_g, preferred_element_type=jnp.float32
        )
        hidden = (jax.nn.silu(gate_up[0]) * gate_up[1]).astype(jnp.bfloat16)
        expert_out = jnp.einsum("ecf,edf->ecd", hidden, down_g, preferred_element_type=jnp.float32)
        slot_rows = slot_token[start_expert * CAP : (start_expert + per_turn) * CAP]
        row_weight = slot_weight[start_expert * CAP : (start_expert + per_turn) * CAP]
        mixture = mixture.at[slot_rows].add(expert_out.reshape(-1, width) * row_weight[:, None])
        saved_acts.append((gate_up, hidden))
    block_out = residual + lax.psum_scatter(
        mixture[:tok_count].astype(jnp.bfloat16), "tensor", scatter_dimension=0, tiled=True
    ).astype(jnp.float32)
    cot_all = lax.all_gather(cotangent, "tensor", axis=0, tiled=True)
    cot_pad = jnp.concatenate([cot_all, jnp.zeros((1, width), jnp.float32)], axis=0)
    slot_cot = (
        (slot_weight[:, None] * cot_pad[slot_token]).astype(jnp.bfloat16).reshape(E, CAP, width)
    )
    back_sum = jnp.zeros((tok_count + 1, width), jnp.float32)
    parts_gate_up = []
    parts_down = []
    for turn_index, start_expert in enumerate(range(0, E, per_turn)):
        gate_up_g, down_g = fetch_experts(w_gate_up, w_down, start_expert, per_turn)
        gate_up, hidden = saved_acts[turn_index]
        gate_vals = gate_up[0]
        up_vals = gate_up[1]
        inputs = expert_in[start_expert : start_expert + per_turn]
        turn_cot = slot_cot[start_expert : start_expert + per_turn]
        down_local = jnp.einsum(
            "ecd,ecf->edf", turn_cot, hidden, preferred_element_type=jnp.float32
        )
        hidden_cot = jnp.einsum(
            "ecd,edf->ecf", turn_cot, down_g, preferred_element_type=jnp.float32
        )
        sigmoid_vals = jax.nn.sigmoid(gate_vals)
        gate_cot = (
            hidden_cot * up_vals * sigmoid_vals * (1.0 + gate_vals * (1.0 - sigmoid_vals))
        ).astype(jnp.bfloat16)
        up_cot = (hidden_cot * gate_vals * sigmoid_vals).astype(jnp.bfloat16)
        both_cot = jnp.stack([gate_cot, up_cot])
        gate_up_local = jnp.einsum(
            "ecd,zecf->ezdf", inputs, both_cot, preferred_element_type=jnp.float32
        )
        input_cot = jnp.einsum(
            "zecf,ezdf->ecd", both_cot, gate_up_g, preferred_element_type=jnp.float32
        )
        slot_rows = slot_token[start_expert * CAP : (start_expert + per_turn) * CAP]
        back_sum = back_sum.at[slot_rows].add(input_cot.reshape(-1, width))
        summed_gate_up, summed_down = (
            lax.psum_scatter(gate_up_local, "dp", scatter_dimension=2, tiled=True),
            lax.psum_scatter(down_local, "dp", scatter_dimension=1, tiled=True),
        )
        parts_gate_up.append(summed_gate_up)
        parts_down.append(summed_down)
    grad_gate_up = jnp.concatenate(parts_gate_up, axis=0)
    grad_down = jnp.concatenate(parts_down, axis=0)
    normed_two_cot = lax.psum_scatter(
        back_sum[:tok_count], "tensor", scatter_dimension=0, tiled=True
    )
    scaled_two = gain_two * normed_two_cot
    residual_cot = (
        cotangent
        + inv_two * scaled_two
        - residual * inv_two**3 * jnp.mean(scaled_two * residual, axis=1, keepdims=True)
    )
    resid_all = lax.all_gather(residual_cot.astype(jnp.bfloat16), "tensor", axis=0, tiled=True)
    out_local = jnp.einsum(
        "td,jtc->jdc", resid_all, attended_flat, preferred_element_type=jnp.float32
    )
    attended_cot = jnp.einsum(
        "td,jdc->jtc", resid_all, out_all, preferred_element_type=jnp.float32
    ).astype(jnp.bfloat16)
    attended_cot = attended_cot.reshape(2, seq_count, SEQ, kv_count, HEAD_SIZE).transpose(
        1, 0, 2, 3, 4
    )
    query_cot, key_cot, value_cot = lax.map(
        attend_back, (queries, keys_rot, values, attended, log_totals, attended_cot)
    )
    query_plain = (
        unrotate(query_cot, cos_table, sine_table)
        .transpose(1, 0, 2, 3, 4)
        .reshape(2, tok_count, kv_count * HEAD_SIZE)
    )
    key_plain = unrotate(key_cot, cos_table, sine_table).reshape(1, tok_count, kv_count * HEAD_SIZE)
    proj_cot = jnp.concatenate(
        [query_plain, key_plain, value_cot.reshape(1, tok_count, kv_count * HEAD_SIZE)], axis=0
    ).astype(jnp.bfloat16)
    attn_local = jnp.einsum("td,ztc->zdc", tokens_one, proj_cot, preferred_element_type=jnp.float32)
    norm_terms = jnp.einsum("ztc,zdc->td", proj_cot, attn_all, preferred_element_type=jnp.float32)
    normed_one_cot = lax.psum_scatter(
        norm_terms.astype(jnp.bfloat16), "tensor", scatter_dimension=0, tiled=True
    ).astype(jnp.float32)
    scaled_one = gain_one * normed_one_cot
    input_grad = (
        residual_cot
        + inv_one * scaled_one
        - block_in * inv_one**3 * jnp.mean(scaled_one * block_in, axis=1, keepdims=True)
    )
    gain_local = jnp.stack(
        [
            jnp.sum(normed_one_cot * block_in * inv_one, axis=0),
            jnp.sum(normed_two_cot * residual * inv_two, axis=0),
        ]
    )
    gain_part, grad_attn, grad_out = (
        lax.psum_scatter(gain_local, "dp", scatter_dimension=1, tiled=True),
        lax.psum_scatter(attn_local, "dp", scatter_dimension=1, tiled=True),
        lax.psum_scatter(out_local, "dp", scatter_dimension=1, tiled=True),
    )
    grad_gains = lax.psum(gain_part, "tensor")
    new_gains, new_m_gains, new_v_gains = adamw_update(
        norm_gains, m_gains, v_gains, grad_gains, rate_gain, 0.0
    )
    new_attn, new_m_attn, new_v_attn = adamw_update(
        attention_weight,
        attention_first_moment,
        attention_second_moment,
        grad_attn,
        rate_matrix,
        decay_matrix,
    )
    new_out, new_m_out, new_v_out = adamw_update(
        output_weight,
        output_first_moment,
        output_second_moment,
        grad_out,
        rate_matrix,
        decay_matrix,
    )
    new_gate_up, new_m_gate_up, new_v_gate_up = adamw_update(
        w_gate_up, m_gate_up, v_gate_up, grad_gate_up, rate_matrix, decay_matrix
    )
    new_down, new_m_down, new_v_down = adamw_update(
        w_down, m_down, v_down, grad_down, rate_matrix, decay_matrix
    )
    return (
        block_out,
        input_grad,
        grad_gains,
        grad_attn,
        grad_out,
        grad_gate_up,
        grad_down,
        new_gains,
        new_attn,
        new_out,
        new_gate_up,
        new_down,
        new_m_gains,
        new_v_gains,
        new_m_attn,
        new_v_attn,
        new_m_out,
        new_v_out,
        new_m_gate_up,
        new_v_gate_up,
        new_m_down,
        new_v_down,
    )


def solution(mesh):
    return jax.shard_map(
        local,
        mesh=mesh,
        in_specs=(
            P(("dp", "tensor"), None),
            P(("dp", "tensor"), None),
            P("dp", None),
            P("dp", None),
            P(None, "dp"),
            P(None, "dp", "tensor"),
            P(None, "dp", "tensor"),
            P(None, None, "dp", "tensor"),
            P(None, "dp", "tensor"),
            P(None, "dp"),
            P(None, "dp"),
            P(None, "dp", "tensor"),
            P(None, "dp", "tensor"),
            P(None, "dp", "tensor"),
            P(None, "dp", "tensor"),
            P(None, None, "dp", "tensor"),
            P(None, None, "dp", "tensor"),
            P(None, "dp", "tensor"),
            P(None, "dp", "tensor"),
        ),
        out_specs=(
            P(("dp", "tensor"), None),
            P(("dp", "tensor"), None),
            P(None, "dp"),
            P(None, "dp", "tensor"),
            P(None, "dp", "tensor"),
            P(None, None, "dp", "tensor"),
            P(None, "dp", "tensor"),
            P(None, "dp"),
            P(None, "dp", "tensor"),
            P(None, "dp", "tensor"),
            P(None, None, "dp", "tensor"),
            P(None, "dp", "tensor"),
            P(None, "dp"),
            P(None, "dp"),
            P(None, "dp", "tensor"),
            P(None, "dp", "tensor"),
            P(None, "dp", "tensor"),
            P(None, "dp", "tensor"),
            P(None, None, "dp", "tensor"),
            P(None, None, "dp", "tensor"),
            P(None, "dp", "tensor"),
            P(None, "dp", "tensor"),
        ),
        check_vma=False,
    )
```

profile of v0, /device:TPU:0, one launch (start us, length us, event | category | flops | bytes accessed | tf_op | source)
XLA Modules:
  0.0 941.3 jit_solution(5812253227274895094)
XLA Ops:
  8.0 10.3 %all_gather.37 = bf16[2,1024]{1,0:T(2,128)(2,1)S(1)} all-gather(bf16[2,128]{1,0:T(2,128)(2,1)S(1)} %convert_element_type.103), channel_id=1, replica_groups=mesh['dp'=8,'tensor'=4] {'dp'}, dimensions={1}, use_global_device_ids=true | all-gather | bytes 4608 | tf_op jit(solution)/shard_map/all_gather | solution.py:161
  23.8 9.8 %all_gather.40 = bf16[2,1024,128]{2,1,0:T(8,128)(2,1)S(1)} all-gather(bf16[2,128,128]{2,1,0:T(8,128)(2,1)S(1)} %convert_element_type.110), channel_id=1, replica_groups=mesh['dp'=8,'tensor'=4] {'dp'}, dimensions={1}, use_global_device_ids=true | all-gather | bytes 589824 | tf_op jit(solution)/shard_map/all_gather | solution.py:163
  34.1 16.2 %all-gather.10.cloned.1.call-done = bf16[512,1024]{1,0:T(8,128)(2,1)} async-done(((bf16[128,1024]{1,0:T(8,128)(2,1)}), bf16[512,1024]{1,0:T(8,128)(2,1)}) %all-gather.10.cloned.1.call-update) | async-done | bytes 1048592 | tf_op jit(solution)/shard_map/all_gather | solution.py:174
  50.3 25.3 %all-gather.12.cloned.1.call-done = bf16[4,1024,128]{1,2,0:T(8,128)(2,1)} async-done(((bf16[4,128,128]{1,2,0:T(8,128)(2,1)}), bf16[4,1024,128]{1,2,0:T(8,128)(2,1)}) %all-gather.12.cloned.1.call-update) | async-done | bytes 1048592 | tf_op jit(solution)/shard_map/all_gather | solution.py:162
  86.5 43.2 %reduce-scatter.14.cloned.1.call-done = f32[128,1024]{1,0:T(8,128)} async-done(((f32[512,1024]{1,0:T(8,128)}), f32[128,1024]{1,0:T(8,128)}) %reduce-scatter.14.cloned.1.call-update) | async-done | bytes 524304 | tf_op jit(solution)/shard_map/reduce_scatter | solution.py:187
  139.9 15.5 %scatter_custom_fusion = s32[4608]{0:T(1024)S(1)} fusion(s32[4096]{0:T(1024)S(1)} %bitcast.271, s32[4096]{0:T(1024)S(1)} %reshape.349, s32[]{:T(128)} %constant.51.clone.1), kind=kCustom, calls=%fused_computation.145 | custom fusion | bytes 18436 | tf_op jit(solution)/shard_map/scatter | solution.py:114
  155.8 16.0 %scatter_custom_fusion.1 = f32[4608]{0:T(1024)S(1)} fusion(s32[4096]{0:T(1024)S(1)} %bitcast.272, f32[4096]{0:T(1024)S(1)} %reshape.357, f32[]{:T(128)} %constant.43.clone.1), kind=kCustom, calls=%fused_computation.143 | custom fusion | bytes 18436 | tf_op jit(solution)/shard_map/scatter | solution.py:115
  171.8 4.1 all-gather.24.cloned.1.call-done
  177.7 15.2 %gather_fusion.1 = f32[4608,1024]{1,0:T(8,128)} fusion(f32[513,1024]{1,0:T(8,128)S(1)} %concatenate.53, s32[5120]{0:T(1024)S(1)} %pad_clamp_fusion), kind=kCustom, calls=%fused_computation.1 | custom fusion | bytes 37767168 | tf_op jit(solution)/shard_map/gather | solution.py:215
  192.9 8.0 multiply_convert_fusion
  200.9 4.8 fusion.72
  207.0 14.9 %gather_fusion = bf16[4608,1024]{1,0:T(8,128)(2,1)} fusion(bf16[513,1024]{1,0:T(8,128)(2,1)S(1)} %concatenate.52, s32[5120]{0:T(1024)S(1)} %pad_clamp_fusion), kind=kCustom, calls=%fused_computation | custom fusion | bytes 18892800 | tf_op jit(solution)/shard_map/gather | solution.py:193
  221.9 8.7 fusion.73
  230.6 12.5 %all-gather.16.cloned.1.call-done = bf16[8,2,1024,128]{3,2,1,0:T(8,128)(2,1)} async-done(((bf16[8,2,128,128]{3,2,1,0:T(8,128)(2,1)}), bf16[8,2,1024,128]{3,2,1,0:T(8,128)(2,1)}) %all-gather.16.cloned.1.call-update) | async-done | bytes 4194320 | tf_op jit(solution)/shard_map/all_gather | solution.py:123
  243.1 5.0 convolution_bitcast_fusion.2
  248.1 25.3 %all-gather.18.cloned.1.call-done = bf16[8,1024,128]{2,1,0:T(8,128)(2,1)} async-done(((bf16[8,128,128]{2,1,0:T(8,128)(2,1)}), bf16[8,1024,128]{2,1,0:T(8,128)(2,1)}) %all-gather.18.cloned.1.call-update) | async-done | bytes 2097168 | tf_op jit(solution)/shard_map/all_gather | solution.py:124
  273.4 4.9 fusion.38
  278.3 5.1 fusion.2
  283.4 24.2 %scatter_custom_fusion.4 = f32[513,1024]{1,0:T(8,128)S(1)} fusion(s32[2304]{0:T(1024)S(1)} %get-tuple-element.209, f32[2304,1024]{1,0:T(8,128)} %bitcast.236, f32[]{:T(128)} %constant.43.clone.1), kind=kCustom, calls=%fused_computation.65 | custom fusion | flops 2359296 | bytes 2101760 | tf_op jit(solution)/shard_map/scatter-add | solution.py:246
  307.5 4.9 all-gather.20.cloned.1.call-done
  312.5 6.4 fusion.13
  318.9 23.9 %all-gather.22.cloned.1.call-done = bf16[8,1024,128]{2,1,0:T(8,128)(2,1)} async-done(((bf16[8,128,128]{2,1,0:T(8,128)(2,1)}), bf16[8,1024,128]{2,1,0:T(8,128)(2,1)}) %all-gather.22.cloned.1.call-update) | async-done | bytes 2097168 | tf_op jit(solution)/shard_map/all_gather | solution.py:124
  342.8 6.3 fusion.39
  349.0 5.1 fusion.7
  354.1 24.3 %scatter_fusion.1 = f32[513,1024]{1,0:T(8,128)S(1)} fusion(f32[513,1024]{1,0:T(8,128)S(1)} %scatter_custom_fusion.4, s32[2304]{0:T(1024)S(1)} %get-tuple-element.208, f32[2304,1024]{1,0:T(8,128)} %bitcast.233), kind=kCustom, calls=%fused_computation.7 | custom fusion | flops 2359296 | bytes 28320768 | tf_op jit(solution)/shard_map/scatter-add | solution.py:246
  382.9 4.3 bitcast_multiply_fusion.1
  387.2 24.2 %scatter_custom_fusion.2 = f32[513,1024]{1,0:T(8,128)S(1)} fusion(s32[2304]{0:T(1024)S(1)} %get-tuple-element.209, f32[2304,1024]{1,0:T(8,128)} %bitcast_multiply_fusion.1, f32[]{:T(128)} %constant.43.clone.1), kind=kCustom, calls=%fused_computation.67 | custom fusion | flops 2359296 | bytes 2101760 | tf_op jit(solution)/shard_map/scatter-add | solution.py:207
  411.5 3.2 fusion.80
  414.7 4.3 bitcast_multiply_fusion
  419.0 24.1 %scatter_fusion = f32[513,1024]{1,0:T(8,128)S(1)} fusion(f32[513,1024]{1,0:T(8,128)S(1)} %scatter_custom_fusion.2, s32[2304]{0:T(1024)S(1)} %get-tuple-element.208, f32[2304,1024]{1,0:T(8,128)} %bitcast_multiply_fusion), kind=kCustom, calls=%fused_computation.5 | custom fusion | flops 2359296 | bytes 28320768 | tf_op jit(solution)/shard_map/scatter-add | solution.py:207
  445.8 26.1 %reduce-scatter.16.cloned.1.call-done = bf16[128,1024]{1,0:T(8,128)(2,1)} async-done(((bf16[512,1024]{1,0:T(8,128)(2,1)}), bf16[128,1024]{1,0:T(8,128)(2,1)}) %reduce-scatter.16.cloned.1.call-update) | async-done | bytes 262160 | tf_op jit(solution)/shard_map/reduce_scatter | solution.py:209
  474.5 26.4 %all-gather.26.cloned.1.call-done = bf16[512,1024]{1,0:T(8,128)(2,1)} async-done(((bf16[128,1024]{1,0:T(8,128)(2,1)}), bf16[512,1024]{1,0:T(8,128)(2,1)}) %all-gather.26.cloned.1.call-update) | async-done | bytes 1048592 | tf_op jit(solution)/shard_map/all_gather | solution.py:264
  511.9 6.3 fusion.82
  519.2 6.4 fusion.83
  528.4 10.1 %reduce-scatter.20.cloned.1.call-done = bf16[128,1024]{1,0:T(8,128)(2,1)} async-done(((bf16[512,1024]{1,0:T(8,128)(2,1)}), bf16[128,1024]{1,0:T(8,128)(2,1)}) %reduce-scatter.20.cloned.1.call-update) | async-done | bytes 262160 | tf_op jit(solution)/shard_map/reduce_scatter | solution.py:288
  543.5 8.6 convolution_bitcast_fusion.1
  553.5 8.1 convolution_bitcast_fusion
  573.0 18.4 %reduce-scatter.30.cloned.1.call-done = f32[8,128,128]{2,1,0:T(8,128)} async-done(((f32[8,1024,128]{2,1,0:T(8,128)}), f32[8,128,128]{2,1,0:T(8,128)}) %reduce-scatter.30.cloned.1.call-update) | async-done | bytes 524304 | tf_op jit(solution)/shard_map/reduce_scatter | solution.py:249
  592.4 53.3 %reduce-scatter.32.cloned.1.call-done = f32[8,128,128]{2,1,0:T(8,128)} async-done(((f32[8,1024,128]{2,1,0:T(8,128)}), f32[8,128,128]{2,1,0:T(8,128)}) %reduce-scatter.32.cloned.1.call-update) | async-done | bytes 524304 | tf_op jit(solution)/shard_map/reduce_scatter | solution.py:249
  646.8 4.1 multiply_subtract_fusion.1
  651.0 34.3 %reduce-scatter.24.cloned.1.call-done = f32[2,128,128]{1,2,0:T(8,128)} async-done(((f32[2,1024,128]{1,2,0:T(8,128)}), f32[2,128,128]{1,2,0:T(8,128)}) %reduce-scatter.24.cloned.1.call-update) | async-done | bytes 131088 | tf_op jit(solution)/shard_map/reduce_scatter | solution.py:306
  692.6 29.8 %reduce-scatter.34.cloned.1.call-done = f32[128,2]{1,0:T(8,128)} async-done(((f32[1024,2]{1,0:T(8,128)}), f32[128,2]{1,0:T(8,128)}) %reduce-scatter.34.cloned.1.call-update) | async-done | bytes 1040
  723.3 11.7 %psum.7 = f32[2,128]{1,0:T(2,128)S(1)} all-reduce(f32[2,128]{1,0:T(2,128)S(1)} %copy.266), channel_id=1, replica_groups=mesh['dp'=8,'tensor'=4] {'tensor'}, use_global_device_ids=true, to_apply=%region_23.24 | all-reduce | flops 256 | bytes 2048 | tf_op jit(solution)/shard_map/psum | solution.py:308
  735.6 31.7 %reduce-scatter.22.cloned.1.call-done = f32[4,128,128]{1,2,0:T(8,128)} async-done(((f32[4,1024,128]{1,2,0:T(8,128)}), f32[4,128,128]{1,2,0:T(8,128)}) %reduce-scatter.22.cloned.1.call-update) | async-done | bytes 262160 | tf_op jit(solution)/shard_map/reduce_scatter | solution.py:305
  771.8 70.2 %reduce-scatter.26.cloned.1.call-done = f32[8,2,128,128]{2,3,1,0:T(8,128)} async-done(((f32[8,2,1024,128]{2,3,1,0:T(8,128)}), f32[8,2,128,128]{2,3,1,0:T(8,128)}) %reduce-scatter.26.cloned.1.call-update) | async-done | bytes 1048592 | tf_op jit(solution)/shard_map/reduce_scatter | solution.py:248
  843.4 73.3 %reduce-scatter.28.cloned.1.call-done = f32[8,2,128,128]{2,3,1,0:T(8,128)} async-done(((f32[8,2,1024,128]{2,3,1,0:T(8,128)}), f32[8,2,128,128]{2,3,1,0:T(8,128)}) %reduce-scatter.28.cloned.1.call-update) | async-done | bytes 1048592 | tf_op jit(solution)/shard_map/reduce_scatter | solution.py:248
  919.8 6.7 multiply_subtract_fusion
  929.4 3.0 copy.243
  (309 shorter events, 97.1 us)
Async XLA Ops:
  7.2 16.6 %copy-start.51 = (f32[2,128,128]{2,1,0:T(8,128)S(1)}, f32[2,128,128]{2,1,0:T(8,128)}, u32[]{:S(2)}) copy-start(f32[2,128,128]{2,1,0:T(8,128)} %param.25) | copy-start | bytes 393220
  7.2 43.1 %all-gather.10.cloned.1.call-start = ((), (), s32[]{:S(2)}) async-start(), calls=%async_computation.11 | async-start | bytes 1310720 | tf_op jit(solution)/shard_map/all_gather | solution.py:174
  18.2 113.1 %copy-start.63 = (f32[1,1024]{1,0:T(1,128)}, f32[1,1024]{1,0:T(1,128)S(1)}, u32[]{:S(2)}) copy-start(f32[1,1024]{1,0:T(1,128)S(1)} %get-tuple-element.210) | copy-start | bytes 12292
  21.8 53.8 %all-gather.12.cloned.1.call-start = ((), (), s32[]{:S(2)}) async-start(), calls=%async_computation.12 | async-start | bytes 1179648 | tf_op jit(solution)/shard_map/all_gather | solution.py:162
  23.7 105.9 %reduce-scatter.14.cloned.1.call-start = ((), (), s32[]{:S(2)}) async-start(), calls=%async_computation.13 | async-start | bytes 2621440 | tf_op jit(solution)/shard_map/reduce_scatter | solution.py:187
  33.7 49.6 %copy-start.13 = (bf16[2,1024,128]{2,1,0:T(8,128)(2,1)}, bf16[2,1024,128]{2,1,0:T(8,128)(2,1)S(1)}, u32[]{:S(2)}) copy-start(bf16[2,1024,128]{2,1,0:T(8,128)(2,1)S(1)} %all_gather.40) | copy-start | bytes 1572868
  33.7 46.4 %copy-start.19 = (pred[512,512]{0,1:T(8,128)(4,1)}, pred[512,512]{0,1:T(8,128)(4,1)S(1)}, u32[]{:S(2)}) copy-start(pred[512,512]{0,1:T(8,128)(4,1)S(1)} %iota_compare_fusion) | copy-start | bytes 786436
  34.1 44.0 %copy-start.38 = (f32[512,32]{0,1:T(8,128)}, f32[512,32]{0,1:T(8,128)S(1)}, u32[]{:S(2)}) copy-start(f32[512,32]{0,1:T(8,128)S(1)} %get-tuple-element.216) | copy-start | bytes 196612
  34.1 44.0 %copy-start.40 = (f32[512,32]{0,1:T(8,128)}, f32[512,32]{0,1:T(8,128)S(1)}, u32[]{:S(2)}) copy-start(f32[512,32]{0,1:T(8,128)S(1)} %get-tuple-element.217) | copy-start | bytes 196612
  84.0 45.6 %copy-start.3 = (f32[128,1024]{1,0:T(8,128)S(1)}, f32[128,1024]{1,0:T(8,128)}, u32[]{:S(2)}) copy-start(f32[128,1024]{1,0:T(8,128)} %param.19) | copy-start | bytes 1572868
  85.8 47.0 %copy-start.9 = (f32[16,2,128,128]{3,2,1,0:T(8,128)S(1)}, f32[16,2,128,128]{3,2,1,0:T(8,128)}, u32[]{:S(2)}) copy-start(f32[16,2,128,128]{3,2,1,0:T(8,128)} %param.26) | copy-start | bytes 6291460
  85.8 90.1 %all-gather.24.cloned.1.call-start = ((), (), s32[]{:S(2)}) async-start(), calls=%async_computation.20 | async-start | bytes 2621440 | tf_op jit(solution)/shard_map/all_gather | solution.py:212
  86.4 119.2 %all-gather.14.cloned.1.call-start = ((), (), s32[]{:S(2)}) async-start(), calls=%async_computation.14 | async-start | bytes 1310720 | tf_op jit(solution)/shard_map/all_gather | solution.py:190
  132.7 110.4 %all-gather.16.cloned.1.call-start = ((), (), s32[]{:S(2)}) async-start(), calls=%async_computation.15 | async-start | bytes 4718592 | tf_op jit(solution)/shard_map/all_gather | solution.py:123
  134.0 139.4 %all-gather.18.cloned.1.call-start = ((), (), s32[]{:S(2)}) async-start(), calls=%async_computation.16 | async-start | bytes 2359296 | tf_op jit(solution)/shard_map/all_gather | solution.py:124
  135.4 20.2 %copy-start.67 = (f32[512,8]{0,1:T(8,128)S(1)}, f32[512,8]{0,1:T(8,128)}, u32[]{:S(2)}) copy-start(f32[512,8]{0,1:T(8,128)} %param.22) | copy-start | bytes 49156
  136.2 176.2 %all-gather.20.cloned.1.call-start = ((), (), s32[]{:S(2)}) async-start(), calls=%async_computation.17 | async-start | bytes 4718592 | tf_op jit(solution)/shard_map/all_gather | solution.py:123
  137.0 205.8 %all-gather.22.cloned.1.call-start = ((), (), s32[]{:S(2)}) async-start(), calls=%async_computation.18 | async-start | bytes 2359296 | tf_op jit(solution)/shard_map/all_gather | solution.py:124
  137.7 306.7 %reduce-scatter.18.cloned.1.call-start = ((), (), s32[]{:S(2)}) async-start(), calls=%async_computation.21 | async-start | bytes 2621440 | tf_op jit(solution)/shard_map/reduce_scatter | solution.py:255
  278.3 5.1 copy-start.25
  278.3 5.1 copy-start.27
  342.8 6.3 copy-start.5
  379.9 91.9 %reduce-scatter.16.cloned.1.call-start = ((), (), s32[]{:S(2)}) async-start(), calls=%async_computation.19 | async-start | bytes 1310720 | tf_op jit(solution)/shard_map/reduce_scatter | solution.py:209
  443.2 28.7 %copy-start.76 = (f32[128]{0:T(128)S(1)}, f32[128]{0:T(128)}, u32[]{:S(2)}) copy-start(f32[128]{0:T(128)} %get-tuple-element.214) | copy-start | bytes 1540
  444.3 27.5 %copy-start.35 = (f32[128,1024]{1,0:T(8,128)S(1)}, f32[128,1024]{1,0:T(8,128)}, u32[]{:S(2)}) copy-start(f32[128,1024]{1,0:T(8,128)} %param.20) | copy-start | bytes 1572868
  444.3 29.9 %copy-start.14 = (bf16[2,1024,128]{2,1,0:T(8,128)(2,1)S(1)}, bf16[2,1024,128]{2,1,0:T(8,128)(2,1)}, u32[]{:S(2)}) copy-start(bf16[2,1024,128]{2,1,0:T(8,128)(2,1)} %copy-done.13) | copy-start | bytes 1572868
  444.4 56.5 %all-gather.26.cloned.1.call-start = ((), (), s32[]{:S(2)}) async-start(), calls=%async_computation.22 | async-start | bytes 1310720 | tf_op jit(solution)/shard_map/all_gather | solution.py:264
  474.2 64.3 %reduce-scatter.20.cloned.1.call-start = ((), (), s32[]{:S(2)}) async-start(), calls=%async_computation.23 | async-start | bytes 1310720 | tf_op jit(solution)/shard_map/reduce_scatter | solution.py:288
  474.5 28.2 %copy-start.12 = (bf16[2,2,512,512]{2,3,0,1:T(8,128)(2,1)S(1)}, bf16[2,2,512,512]{2,3,0,1:T(8,128)(2,1)}, u32[]{:S(2)}) copy-start(bf16[2,2,512,512]{2,3,0,1:T(8,128)(2,1)} %copy-done.11) | copy-start | bytes 6291460
  511.7 79.7 %reduce-scatter.30.cloned.1.call-start = ((), (), s32[]{:S(2)}) async-start(), calls=%async_computation.28 | async-start | bytes 4718592 | tf_op jit(solution)/shard_map/reduce_scatter | solution.py:249
  518.2 127.5 %reduce-scatter.32.cloned.1.call-start = ((), (), s32[]{:S(2)}) async-start(), calls=%async_computation.29 | async-start | bytes 4718592 | tf_op jit(solution)/shard_map/reduce_scatter | solution.py:249
  525.7 12.9 %copy-start.4 = (f32[128,1024]{1,0:T(8,128)S(1)}, f32[128,1024]{1,0:T(8,128)}, u32[]{:S(2)}) copy-start(f32[128,1024]{1,0:T(8,128)} %param.19) | copy-start | bytes 1572868
  525.7 12.8 %copy-start.62 = (f32[1,1024]{1,0:T(1,128)S(1)}, f32[1,1024]{1,0:T(1,128)}, u32[]{:S(2)}) copy-start(f32[1,1024]{1,0:T(1,128)} %copy-done.61) | copy-start | bytes 12292
  525.7 12.8 %copy-start.71 = (f32[128]{0:T(128)S(1)}, f32[128]{0:T(128)}, u32[]{:S(2)}) copy-start(f32[128]{0:T(128)} %copy-done.70) | copy-start | bytes 1540
  525.7 15.6 %copy-start.42 = (bf16[512,1024]{1,0:T(8,128)(2,1)S(1)}, bf16[512,1024]{1,0:T(8,128)(2,1)}, u32[]{:S(2)}) copy-start(bf16[512,1024]{1,0:T(8,128)(2,1)} %all-gather.10.cloned.1.call-done) | copy-start | bytes 3145732
  525.7 159.6 %reduce-scatter.24.cloned.1.call-start = ((), (), s32[]{:S(2)}) async-start(), calls=%async_computation.25 | async-start | bytes 1179648 | tf_op jit(solution)/shard_map/reduce_scatter | solution.py:306
  528.3 194.0 %reduce-scatter.34.cloned.1.call-start = ((), (), s32[]{:S(2)}) async-start(), calls=%async_computation.30 | async-start | bytes 589824
  541.3 226.0 %reduce-scatter.22.cloned.1.call-start = ((), (), s32[]{:S(2)}) async-start(), calls=%async_computation.24 | async-start | bytes 2359296 | tf_op jit(solution)/shard_map/reduce_scatter | solution.py:305
  543.4 298.6 %reduce-scatter.26.cloned.1.call-start = ((), (), s32[]{:S(2)}) async-start(), calls=%async_computation.26 | async-start | bytes 9437184 | tf_op jit(solution)/shard_map/reduce_scatter | solution.py:248
  552.1 364.6 %reduce-scatter.28.cloned.1.call-start = ((), (), s32[]{:S(2)}) async-start(), calls=%async_computation.27 | async-start | bytes 9437184 | tf_op jit(solution)/shard_map/reduce_scatter | solution.py:248
  570.0 76.8 %copy-start.15 = (f32[16,128,128]{2,1,0:T(8,128)S(1)}, f32[16,128,128]{2,1,0:T(8,128)}, u32[]{:S(2)}) copy-start(f32[16,128,128]{2,1,0:T(8,128)} %param.27) | copy-start | bytes 3145732
  650.9 40.0 %copy-start.36 = (f32[128,1024]{1,0:T(8,128)S(1)}, f32[128,1024]{1,0:T(8,128)}, u32[]{:S(2)}) copy-start(f32[128,1024]{1,0:T(8,128)} %get-tuple-element.178) | copy-start | bytes 1572868
  650.9 40.0 %copy-start.44 = (bf16[128,1024]{1,0:T(8,128)(2,1)S(1)}, bf16[128,1024]{1,0:T(8,128)(2,1)}, u32[]{:S(2)}) copy-start(bf16[128,1024]{1,0:T(8,128)(2,1)} %reduce-scatter.20.cloned.1.call-done) | copy-start | bytes 786436
  650.9 84.0 %copy-start.73 = (f32[2,128]{1,0:T(2,128)S(1)}, f32[2,128]{1,0:T(2,128)}, u32[]{:S(2)}) copy-start(f32[2,128]{1,0:T(2,128)} %param.23) | copy-start | bytes 3076
  651.0 84.0 %copy-start.74 = (f32[2,128]{1,0:T(2,128)S(1)}, f32[2,128]{1,0:T(2,128)}, u32[]{:S(2)}) copy-start(f32[2,128]{1,0:T(2,128)} %param.28) | copy-start | bytes 3076
  651.0 116.3 %copy-start.24 = (f32[4,128,128]{1,2,0:T(8,128)S(1)}, f32[4,128,128]{1,2,0:T(8,128)}, u32[]{:S(2)}) copy-start(f32[4,128,128]{1,2,0:T(8,128)} %copy-done.23) | copy-start | bytes 786436
  685.3 49.7 %copy-start.75 = (f32[2,128]{1,0:T(2,128)S(1)}, f32[2,128]{1,0:T(2,128)}, u32[]{:S(2)}) copy-start(f32[2,128]{1,0:T(2,128)} %param.29) | copy-start | bytes 3076
  735.0 108.4 %copy-start.72 = (f32[2,128]{1,0:T(2,128)}, f32[2,128]{1,0:T(2,128)S(1)}, u32[]{:S(2)}) copy-start(f32[2,128]{1,0:T(2,128)S(1)} %psum.7) | copy-start | bytes 3076
  (49 other events, 91.7 us)
Sparse Core Ops, SparseCore 0:
  21.9 28.2 all-gather.9
  52.7 22.8 all-gather.11
  85.9 43.6 reduce-scatter.13
  131.0 44.8 all-gather.23
  177.9 26.7 all-gather.13
  207.1 35.9 all-gather.15
  245.6 27.7 all-gather.17
  275.9 36.5 all-gather.19
  315.0 27.7 all-gather.21
  380.1 43.5 reduce-scatter.17
  444.5 27.3 reduce-scatter.15
  474.4 26.4 all-gather.25
  511.8 26.6 reduce-scatter.19
  541.7 49.5 reduce-scatter.29
  594.6 51.0 reduce-scatter.31
  649.3 35.9 reduce-scatter.23
  688.2 34.0 reduce-scatter.33
  726.1 41.1 reduce-scatter.21
  770.7 71.2 reduce-scatter.25
  845.3 71.2 reduce-scatter.27
where the time goes:
time: 950 us; the launch traced here: 941 us
  waiting for transfers between devices  531 us (56%)
  other arithmetic  148 us (16%)
  local copies, waits for them, and re-layouts  130 us (14%)
  matrix products  83.7 us (9%)
  blocking collectives  31.8 us (3%)
  between operations  15.7 us (2%)
    reduce_scatter x2, waiting for transfers between devices, local(): lax.psum_scatter(gate_up_local, 'dp', scatter_dimension=2, tiled=True)  144 us
    reduce_scatter x2, waiting for transfers between devices, local(): lax.psum_scatter(down_local, 'dp', scatter_dimension=1, tiled=True)  71.7 us
    all_gather x2, waiting for transfers between devices, fetch_experts(): lax.all_gather(down_part, 'dp', axis=1, tiled=True)  49.2 us
    scatter-add x2, other arithmetic, local(): back_sum = back_sum.at[slot_rows].add(input_cot.reshape(-1, width))  48.5 us
    scatter-add x2, other arithmetic, local(): mixture.at[slot_rows]  48.4 us
    unnamed x180, local copies, waits for them, and re-layouts  43.3 us
    reduce_scatter x1, waiting for transfers between devices, local(): lax.psum_scatter(partial_value, 'tensor', scatter_dimension=0, tiled=True)  43.2 us
    reduce_scatter x1, waiting for transfers between devices, local(): lax.psum_scatter(out_local, 'dp', scatter_dimension=1, tiled=True)  34.3 us
  transfers between devices with their start and end apart: 20, of which 18 were waited for; matrix products, arithmetic and copies ran while one was open for 29% of the time, Pallas kernels for 0%

commit v1 on v0

--- a/solution.py
+++ b/solution.py
@@ -18,6 +18,18 @@
 rope_base = 10000.0
 
 
+def gather_by_bits(array, axis, dim):
+    ways, here, lap = (lax.axis_size(axis), lax.axis_index(axis), array.shape[dim])
+    line, have = (array, 1)
+    while have < ways:
+        line = jnp.concatenate(
+            [line, lax.ppermute(line, axis, [(d, (d - have) % ways) for d in range(ways)])],
+            axis=dim,
+        )
+        have = 2 * have
+    return jnp.roll(line, here * lap, axis=dim)
+
+
 def rope_tables(length, width):
     half_width = width // 2
     frequency = rope_base ** (-(2.0 * jnp.arange(half_width, dtype=jnp.float32)) / width)
@@ -121,7 +133,7 @@
     down_part = w_down[start_expert : start_expert + per_turn].astype(jnp.bfloat16)
     return (
         lax.all_gather(gate_up_part, "dp", axis=2, tiled=True),
-        lax.all_gather(down_part, "dp", axis=1, tiled=True),
+        gather_by_bits(down_part, "dp", 1),
     )
 
 

time: 950 us -> 922 us (0.971)
  waiting for transfers between devices: 531 us -> 484 us
  other arithmetic: 148 us -> 164 us
    all_gather x2 -> x0, waiting for transfers between devices: 49.2 us -> none  [fetch_experts(): lax.all_gather(down_part, 'dp', axis=1, tiled=True)]
    ppermute x0 -> x6, waiting for transfers between devices: none -> 18.5 us  [gather_by_bits(): lax.ppermute(line, axis, [(d, (d - have) % ways) for d in range(ways)])]
    all_gather x2, waiting for transfers between devices: 17.5 us -> 0.02 us  [fetch_experts(): lax.all_gather(gate_up_part, 'dp', axis=2, tiled=True)]
    concatenate x0 -> x6, other arithmetic: none -> 16.2 us  [the longest x2 13.2 us: gather_by_bits(): return jnp.roll(line, here * lap, axis=dim)]
    unnamed x21 -> x19, waiting for transfers between devices: 32 us -> 30.6 us
    unnamed x180 -> x186, local copies, waits for them, and re-layouts: 43.3 us -> 43.8 us
  transfers between devices with their start and end apart: 20 -> 24, of which waited for: 18 -> 17; matrix products, arithmetic and copies ran while one was open for 29% -> 31% of each run, Pallas kernels for 0% -> 0%
where the time goes in v1:
time: 922 us; the launch traced here: 912 us
  waiting for transfers between devices  484 us (52%)
  other arithmetic  164 us (18%)
  local copies, waits for them, and re-layouts  130 us (14%)
  matrix products  79.1 us (9%)
  blocking collectives  32 us (3%)
  between operations  16 us (2%)
    reduce_scatter x2, waiting for transfers between devices, local(): lax.psum_scatter(gate_up_local, 'dp', scatter_dimension=2, tiled=True)  143 us
    reduce_scatter x2, waiting for transfers between devices, local(): lax.psum_scatter(down_local, 'dp', scatter_dimension=1, tiled=True)  71.8 us
    scatter-add x2, other arithmetic, local(): back_sum = back_sum.at[slot_rows].add(input_cot.reshape(-1, width))  48.2 us
    scatter-add x2, other arithmetic, local(): mixture.at[slot_rows]  48.1 us
    unnamed x186, local copies, waits for them, and re-layouts  43.8 us
    reduce_scatter x1, waiting for transfers between devices, local(): lax.psum_scatter(partial_value, 'tensor', scatter_dimension=0, tiled=True)  43.2 us
    reduce_scatter x1, waiting for transfers between devices, local(): lax.psum_scatter(out_local, 'dp', scatter_dimension=1, tiled=True)  34.3 us
    reduce_scatter x1, waiting for transfers between devices, local(): lax.psum_scatter(mixture[:tok_count].astype(jnp.bfloat16), 'tensor', scat...  32.5 us
  transfers between devices with their start and end apart: 24, of which 17 were waited for; matrix products, arithmetic and copies ran while one was open for 31% of the time, Pallas kernels for 0%

profile of v1, /device:TPU:0, one launch (start us, length us, event | category | flops | bytes accessed | tf_op | source)
XLA Modules:
  0.0 912.4 jit_solution(10261793296052355082)
XLA Ops:
  8.0 10.3 %all_gather.29 = bf16[2,1024]{1,0:T(2,128)(2,1)S(1)} all-gather(bf16[2,128]{1,0:T(2,128)(2,1)S(1)} %convert_element_type.103), channel_id=1, replica_groups=mesh['dp'=8,'tensor'=4] {'dp'}, dimensions={1}, use_global_device_ids=true | all-gather | bytes 4608 | tf_op jit(solution)/shard_map/all_gather | solution.py:173
  23.8 9.8 %all_gather.32 = bf16[2,1024,128]{2,1,0:T(8,128)(2,1)S(1)} all-gather(bf16[2,128,128]{2,1,0:T(8,128)(2,1)S(1)} %convert_element_type.110), channel_id=1, replica_groups=mesh['dp'=8,'tensor'=4] {'dp'}, dimensions={1}, use_global_device_ids=true | all-gather | bytes 589824 | tf_op jit(solution)/shard_map/all_gather | solution.py:175
  34.1 16.1 %all-gather.8.cloned.1.call-done = bf16[512,1024]{1,0:T(8,128)(2,1)} async-done(((bf16[128,1024]{1,0:T(8,128)(2,1)}), bf16[512,1024]{1,0:T(8,128)(2,1)}) %all-gather.8.cloned.1.call-update) | async-done | bytes 1048592 | tf_op jit(solution)/shard_map/all_gather | solution.py:186
  50.3 25.3 %all-gather.10.cloned.1.call-done = bf16[4,1024,128]{1,2,0:T(8,128)(2,1)} async-done(((bf16[4,128,128]{1,2,0:T(8,128)(2,1)}), bf16[4,1024,128]{1,2,0:T(8,128)(2,1)}) %all-gather.10.cloned.1.call-update) | async-done | bytes 1048592 | tf_op jit(solution)/shard_map/all_gather | solution.py:174
  86.5 43.2 %reduce-scatter.14.cloned.1.call-done = f32[128,1024]{1,0:T(8,128)} async-done(((f32[512,1024]{1,0:T(8,128)}), f32[128,1024]{1,0:T(8,128)}) %reduce-scatter.14.cloned.1.call-update) | async-done | bytes 524304 | tf_op jit(solution)/shard_map/reduce_scatter | solution.py:199
  145.4 10.3 %collective-permute-done.1 = bf16[8,256,128]{2,1,0:T(8,128)(2,1)S(1)} collective-permute-done((bf16[8,256,128]{2,1,0:T(8,128)(2,1)S(1)}, bf16[8,256,128]{2,1,0:T(8,128)(2,1)S(1)}, u32[]{:S(2)}, u32[]{:S(2)}) %collective-permute-start.1) | collective-permute-done | bytes 524320 | tf_op jit(solution)/shard_map/ppermute | solution.py:26
  158.0 15.5 %scatter_custom_fusion = s32[4608]{0:T(1024)S(1)} fusion(s32[4096]{0:T(1024)S(1)} %bitcast.271, s32[4096]{0:T(1024)S(1)} %reshape.349, s32[]{:T(128)} %constant.65.clone.1), kind=kCustom, calls=%fused_computation.179 | custom fusion | bytes 18436 | tf_op jit(solution)/shard_map/scatter | solution.py:126
  175.9 16.1 %scatter_custom_fusion.1 = f32[4608]{0:T(1024)S(1)} fusion(s32[4096]{0:T(1024)S(1)} %bitcast.272, f32[4096]{0:T(1024)S(1)} %reshape.357, f32[]{:T(128)} %constant.57.clone.1), kind=kCustom, calls=%fused_computation.177 | custom fusion | bytes 18436 | tf_op jit(solution)/shard_map/scatter | solution.py:127
  192.0 6.9 fusion.21
  198.9 5.6 collective-permute-done.5
  204.5 6.3 fusion.14
  212.6 15.2 %gather_fusion.1 = f32[4608,1024]{1,0:T(8,128)} fusion(f32[513,1024]{1,0:T(8,128)S(1)} %concatenate.94, s32[5120]{0:T(1024)S(1)} %pad_clamp_fusion), kind=kCustom, calls=%fused_computation.1 | custom fusion | bytes 37767168 | tf_op jit(solution)/shard_map/gather | solution.py:227
  227.7 8.3 multiply_convert_fusion
  236.0 4.8 fusion.86
  242.2 15.1 %gather_fusion = bf16[4608,1024]{1,0:T(8,128)(2,1)} fusion(bf16[513,1024]{1,0:T(8,128)(2,1)S(1)} %concatenate.87, s32[5120]{0:T(1024)S(1)} %pad_clamp_fusion), kind=kCustom, calls=%fused_computation | custom fusion | bytes 18892800 | tf_op jit(solution)/shard_map/gather | solution.py:205
  257.3 8.5 fusion.87
  265.9 5.8 convolution_bitcast_fusion.2
  274.4 5.1 fusion.2
  279.5 24.1 %scatter_custom_fusion.4 = f32[513,1024]{1,0:T(8,128)S(1)} fusion(s32[2304]{0:T(1024)S(1)} %get-tuple-element.210, f32[2304,1024]{1,0:T(8,128)} %bitcast.236, f32[]{:T(128)} %constant.57.clone.1), kind=kCustom, calls=%fused_computation.95 | custom fusion | flops 2359296 | bytes 2101760 | tf_op jit(solution)/shard_map/scatter-add | solution.py:258
  303.7 5.1 fusion.27
  308.8 5.1 fusion.53
  313.9 5.1 fusion.7
  319.0 24.1 %scatter_fusion.1 = f32[513,1024]{1,0:T(8,128)S(1)} fusion(f32[513,1024]{1,0:T(8,128)S(1)} %scatter_custom_fusion.4, s32[2304]{0:T(1024)S(1)} %get-tuple-element.209, f32[2304,1024]{1,0:T(8,128)} %bitcast.233), kind=kCustom, calls=%fused_computation.7 | custom fusion | flops 2359296 | bytes 28320768 | tf_op jit(solution)/shard_map/scatter-add | solution.py:258
  347.6 4.3 bitcast_multiply_fusion.1
  352.0 23.8 %scatter_custom_fusion.2 = f32[513,1024]{1,0:T(8,128)S(1)} fusion(s32[2304]{0:T(1024)S(1)} %get-tuple-element.210, f32[2304,1024]{1,0:T(8,128)} %bitcast_multiply_fusion.1, f32[]{:T(128)} %constant.57.clone.1), kind=kCustom, calls=%fused_computation.97 | custom fusion | flops 2359296 | bytes 2101760 | tf_op jit(solution)/shard_map/scatter-add | solution.py:219
  375.8 3.2 fusion.94
  379.0 4.3 bitcast_multiply_fusion
  383.3 24.3 %scatter_fusion = f32[513,1024]{1,0:T(8,128)S(1)} fusion(f32[513,1024]{1,0:T(8,128)S(1)} %scatter_custom_fusion.2, s32[2304]{0:T(1024)S(1)} %get-tuple-element.209, f32[2304,1024]{1,0:T(8,128)} %bitcast_multiply_fusion), kind=kCustom, calls=%fused_computation.5 | custom fusion | flops 2359296 | bytes 28320768 | tf_op jit(solution)/shard_map/scatter-add | solution.py:219
  410.2 32.5 %reduce-scatter.16.cloned.1.call-done = bf16[128,1024]{1,0:T(8,128)(2,1)} async-done(((bf16[512,1024]{1,0:T(8,128)(2,1)}), bf16[128,1024]{1,0:T(8,128)(2,1)}) %reduce-scatter.16.cloned.1.call-update) | async-done | bytes 262160 | tf_op jit(solution)/shard_map/reduce_scatter | solution.py:221
  445.4 26.3 %all-gather.20.cloned.1.call-done = bf16[512,1024]{1,0:T(8,128)(2,1)} async-done(((bf16[128,1024]{1,0:T(8,128)(2,1)}), bf16[512,1024]{1,0:T(8,128)(2,1)}) %all-gather.20.cloned.1.call-update) | async-done | bytes 1048592 | tf_op jit(solution)/shard_map/all_gather | solution.py:276
  479.6 2.9 bitcast_convert_fusion
  482.6 6.3 fusion.96
  490.0 6.4 fusion.97
  499.2 10.3 %reduce-scatter.20.cloned.1.call-done = bf16[128,1024]{1,0:T(8,128)(2,1)} async-done(((bf16[512,1024]{1,0:T(8,128)(2,1)}), bf16[128,1024]{1,0:T(8,128)(2,1)}) %reduce-scatter.20.cloned.1.call-update) | async-done | bytes 262160 | tf_op jit(solution)/shard_map/reduce_scatter | solution.py:300
  514.4 8.6 convolution_bitcast_fusion.1
  524.4 8.1 convolution_bitcast_fusion
  540.9 3.0 copy.230
  543.8 18.4 %reduce-scatter.30.cloned.1.call-done = f32[8,128,128]{2,1,0:T(8,128)} async-done(((f32[8,1024,128]{2,1,0:T(8,128)}), f32[8,128,128]{2,1,0:T(8,128)}) %reduce-scatter.30.cloned.1.call-update) | async-done | bytes 524304 | tf_op jit(solution)/shard_map/reduce_scatter | solution.py:261
  563.3 53.4 %reduce-scatter.32.cloned.1.call-done = f32[8,128,128]{2,1,0:T(8,128)} async-done(((f32[8,1024,128]{2,1,0:T(8,128)}), f32[8,128,128]{2,1,0:T(8,128)}) %reduce-scatter.32.cloned.1.call-update) | async-done | bytes 524304 | tf_op jit(solution)/shard_map/reduce_scatter | solution.py:261
  617.9 4.1 multiply_subtract_fusion.1
  622.0 34.3 %reduce-scatter.24.cloned.1.call-done = f32[2,128,128]{1,2,0:T(8,128)} async-done(((f32[2,1024,128]{1,2,0:T(8,128)}), f32[2,128,128]{1,2,0:T(8,128)}) %reduce-scatter.24.cloned.1.call-update) | async-done | bytes 131088 | tf_op jit(solution)/shard_map/reduce_scatter | solution.py:318
  663.6 29.8 %reduce-scatter.34.cloned.1.call-done = f32[128,2]{1,0:T(8,128)} async-done(((f32[1024,2]{1,0:T(8,128)}), f32[128,2]{1,0:T(8,128)}) %reduce-scatter.34.cloned.1.call-update) | async-done | bytes 1040
  694.3 11.9 %psum.7 = f32[2,128]{1,0:T(2,128)S(1)} all-reduce(f32[2,128]{1,0:T(2,128)S(1)} %copy.266), channel_id=1, replica_groups=mesh['dp'=8,'tensor'=4] {'tensor'}, use_global_device_ids=true, to_apply=%region_23.25 | all-reduce | flops 256 | bytes 2048 | tf_op jit(solution)/shard_map/psum | solution.py:320
  706.9 31.4 %reduce-scatter.22.cloned.1.call-done = f32[4,128,128]{1,2,0:T(8,128)} async-done(((f32[4,1024,128]{1,2,0:T(8,128)}), f32[4,128,128]{1,2,0:T(8,128)}) %reduce-scatter.22.cloned.1.call-update) | async-done | bytes 262160 | tf_op jit(solution)/shard_map/reduce_scatter | solution.py:317
  742.9 70.1 %reduce-scatter.26.cloned.1.call-done = f32[8,2,128,128]{2,3,1,0:T(8,128)} async-done(((f32[8,2,1024,128]{2,3,1,0:T(8,128)}), f32[8,2,128,128]{2,3,1,0:T(8,128)}) %reduce-scatter.26.cloned.1.call-update) | async-done | bytes 1048592 | tf_op jit(solution)/shard_map/reduce_scatter | solution.py:260
  814.2 73.3 %reduce-scatter.28.cloned.1.call-done = f32[8,2,128,128]{2,3,1,0:T(8,128)} async-done(((f32[8,2,1024,128]{2,3,1,0:T(8,128)}), f32[8,2,128,128]{2,3,1,0:T(8,128)}) %reduce-scatter.28.cloned.1.call-update) | async-done | bytes 1048592 | tf_op jit(solution)/shard_map/reduce_scatter | solution.py:260
  890.7 6.7 multiply_subtract_fusion
  900.2 3.0 copy.243
  (327 shorter events, 103.6 us)
Async XLA Ops:
  7.2 16.6 %copy-start.54 = (f32[2,128,128]{2,1,0:T(8,128)S(1)}, f32[2,128,128]{2,1,0:T(8,128)}, u32[]{:S(2)}) copy-start(f32[2,128,128]{2,1,0:T(8,128)} %param.27) | copy-start | bytes 393220
  7.2 43.1 %all-gather.8.cloned.1.call-start = ((), (), s32[]{:S(2)}) async-start(), calls=%async_computation.11 | async-start | bytes 1310720 | tf_op jit(solution)/shard_map/all_gather | solution.py:186
  18.2 113.2 %copy-start.66 = (f32[1,1024]{1,0:T(1,128)}, f32[1,1024]{1,0:T(1,128)S(1)}, u32[]{:S(2)}) copy-start(f32[1,1024]{1,0:T(1,128)S(1)} %get-tuple-element.211) | copy-start | bytes 12292
  21.8 53.8 %all-gather.10.cloned.1.call-start = ((), (), s32[]{:S(2)}) async-start(), calls=%async_computation.12 | async-start | bytes 1179648 | tf_op jit(solution)/shard_map/all_gather | solution.py:174
  23.7 105.9 %reduce-scatter.14.cloned.1.call-start = ((), (), s32[]{:S(2)}) async-start(), calls=%async_computation.13 | async-start | bytes 2621440 | tf_op jit(solution)/shard_map/reduce_scatter | solution.py:199
  33.7 49.6 %copy-start.17 = (bf16[2,1024,128]{2,1,0:T(8,128)(2,1)}, bf16[2,1024,128]{2,1,0:T(8,128)(2,1)S(1)}, u32[]{:S(2)}) copy-start(bf16[2,1024,128]{2,1,0:T(8,128)(2,1)S(1)} %all_gather.32) | copy-start | bytes 1572868
  33.8 46.4 %copy-start.23 = (pred[512,512]{0,1:T(8,128)(4,1)}, pred[512,512]{0,1:T(8,128)(4,1)S(1)}, u32[]{:S(2)}) copy-start(pred[512,512]{0,1:T(8,128)(4,1)S(1)} %iota_compare_fusion) | copy-start | bytes 786436
  34.1 44.0 %copy-start.41 = (f32[512,32]{0,1:T(8,128)}, f32[512,32]{0,1:T(8,128)S(1)}, u32[]{:S(2)}) copy-start(f32[512,32]{0,1:T(8,128)S(1)} %get-tuple-element.217) | copy-start | bytes 196612
  34.1 44.0 %copy-start.43 = (f32[512,32]{0,1:T(8,128)}, f32[512,32]{0,1:T(8,128)S(1)}, u32[]{:S(2)}) copy-start(f32[512,32]{0,1:T(8,128)S(1)} %get-tuple-element.218) | copy-start | bytes 196612
  84.0 45.6 %copy-start.4 = (f32[128,1024]{1,0:T(8,128)S(1)}, f32[128,1024]{1,0:T(8,128)}, u32[]{:S(2)}) copy-start(f32[128,1024]{1,0:T(8,128)} %param.21) | copy-start | bytes 1572868
  85.8 47.0 %copy-start.10 = (f32[16,2,128,128]{3,2,1,0:T(8,128)S(1)}, f32[16,2,128,128]{3,2,1,0:T(8,128)}, u32[]{:S(2)}) copy-start(f32[16,2,128,128]{3,2,1,0:T(8,128)} %param.28) | copy-start | bytes 6291460
  85.9 125.0 %all-gather.18.cloned.1.call-start = ((), (), s32[]{:S(2)}) async-start(), calls=%async_computation.18 | async-start | bytes 2621440 | tf_op jit(solution)/shard_map/all_gather | solution.py:224
  86.4 154.4 %all-gather.12.cloned.1.call-start = ((), (), s32[]{:S(2)}) async-start(), calls=%async_computation.14 | async-start | bytes 1310720 | tf_op jit(solution)/shard_map/all_gather | solution.py:202
  132.8 133.1 %all-gather.14.cloned.1.call-start = ((), (), s32[]{:S(2)}) async-start(), calls=%async_computation.15 | async-start | bytes 4718592 | tf_op jit(solution)/shard_map/all_gather | solution.py:135
  134.0 169.6 %all-gather.16.cloned.1.call-start = ((), (), s32[]{:S(2)}) async-start(), calls=%async_computation.16 | async-start | bytes 4718592 | tf_op jit(solution)/shard_map/all_gather | solution.py:135
  135.5 5.4 collective-permute-start
  136.9 6.7 collective-permute-start.3
  138.0 270.9 %reduce-scatter.18.cloned.1.call-start = ((), (), s32[]{:S(2)}) async-start(), calls=%async_computation.19 | async-start | bytes 2621440 | tf_op jit(solution)/shard_map/reduce_scatter | solution.py:267
  140.9 14.9 %collective-permute-start.1 = (bf16[8,256,128]{2,1,0:T(8,128)(2,1)S(1)}, bf16[8,256,128]{2,1,0:T(8,128)(2,1)S(1)}, u32[]{:S(2)}, u32[]{:S(2)}) collective-permute-start(bf16[8,256,128]{2,1,0:T(8,128)(2,1)S(1)} %pad_maximum_fusion.4), channel_id=1, source_target_pairs={{0,24},{4,28},{8,0},{12,4},{16,8},{20,12},{24,16},{28,20},{1,25},{... | collective-permute-start | bytes 1572872 | tf_op jit(solution)/shard_map/ppermute | solution.py:26
  144.5 31.2 %copy-start.70 = (f32[512,8]{0,1:T(8,128)S(1)}, f32[512,8]{0,1:T(8,128)}, u32[]{:S(2)}) copy-start(f32[512,8]{0,1:T(8,128)} %param.24) | copy-start | bytes 49156
  144.5 29.1 %collective-permute-start.4 = (bf16[8,256,128]{2,1,0:T(8,128)(2,1)}, bf16[8,256,128]{2,1,0:T(8,128)(2,1)S(1)}, u32[]{:S(2)}, u32[]{:S(2)}) collective-permute-start(bf16[8,256,128]{2,1,0:T(8,128)(2,1)} %pad_maximum_fusion.5), channel_id=1, source_target_pairs={{0,24},{4,28},{8,0},{12,4},{16,8},{20,12},{24,16},{28,20},{1,25},{... | collective-permute-start | bytes 1572872 | tf_op jit(solution)/shard_map/ppermute | solution.py:26
  156.7 35.3 %collective-permute-start.2 = (bf16[8,512,128]{2,1,0:T(8,128)(2,1)}, bf16[8,512,128]{2,1,0:T(8,128)(2,1)S(1)}, u32[]{:S(2)}, u32[]{:S(2)}) collective-permute-start(bf16[8,512,128]{2,1,0:T(8,128)(2,1)} %pad_maximum_fusion.2), channel_id=1, source_target_pairs={{0,16},{4,20},{8,24},{12,28},{16,0},{20,4},{24,8},{28,12},{1,17},{... | collective-permute-start | bytes 3145736 | tf_op jit(solution)/shard_map/ppermute | solution.py:26
  174.6 29.9 %collective-permute-start.5 = (bf16[8,512,128]{2,1,0:T(8,128)(2,1)}, bf16[8,512,128]{2,1,0:T(8,128)(2,1)}, u32[]{:S(2)}, u32[]{:S(2)}) collective-permute-start(bf16[8,512,128]{2,1,0:T(8,128)(2,1)} %pad_maximum_fusion.3), channel_id=1, source_target_pairs={{0,16},{4,20},{8,24},{12,28},{16,0},{20,4},{24,8},{28,12},{1,17},{... | collective-permute-start | bytes 3145736 | tf_op jit(solution)/shard_map/ppermute | solution.py:26
  344.7 98.1 %reduce-scatter.16.cloned.1.call-start = ((), (), s32[]{:S(2)}) async-start(), calls=%async_computation.17 | async-start | bytes 1310720 | tf_op jit(solution)/shard_map/reduce_scatter | solution.py:221
  407.6 35.1 %copy-start.79 = (f32[128]{0:T(128)S(1)}, f32[128]{0:T(128)}, u32[]{:S(2)}) copy-start(f32[128]{0:T(128)} %get-tuple-element.215) | copy-start | bytes 1540
  408.8 34.0 %copy-start.39 = (f32[128,1024]{1,0:T(8,128)S(1)}, f32[128,1024]{1,0:T(8,128)}, u32[]{:S(2)}) copy-start(f32[128,1024]{1,0:T(8,128)} %param.22) | copy-start | bytes 1572868
  408.8 36.4 %copy-start.18 = (bf16[2,1024,128]{2,1,0:T(8,128)(2,1)S(1)}, bf16[2,1024,128]{2,1,0:T(8,128)(2,1)}, u32[]{:S(2)}) copy-start(bf16[2,1024,128]{2,1,0:T(8,128)(2,1)} %copy-done.17) | copy-start | bytes 1572868
  408.8 63.0 %all-gather.20.cloned.1.call-start = ((), (), s32[]{:S(2)}) async-start(), calls=%async_computation.20 | async-start | bytes 1310720 | tf_op jit(solution)/shard_map/all_gather | solution.py:276
  445.1 64.3 %reduce-scatter.20.cloned.1.call-start = ((), (), s32[]{:S(2)}) async-start(), calls=%async_computation.21 | async-start | bytes 1310720 | tf_op jit(solution)/shard_map/reduce_scatter | solution.py:300
  445.4 28.2 %copy-start.13 = (bf16[2,2,512,512]{2,3,0,1:T(8,128)(2,1)S(1)}, bf16[2,2,512,512]{2,3,0,1:T(8,128)(2,1)}, u32[]{:S(2)}) copy-start(bf16[2,2,512,512]{2,3,0,1:T(8,128)(2,1)} %copy-done.12) | copy-start | bytes 6291460
  482.6 79.7 %reduce-scatter.30.cloned.1.call-start = ((), (), s32[]{:S(2)}) async-start(), calls=%async_computation.26 | async-start | bytes 4718592 | tf_op jit(solution)/shard_map/reduce_scatter | solution.py:261
  489.0 127.8 %reduce-scatter.32.cloned.1.call-start = ((), (), s32[]{:S(2)}) async-start(), calls=%async_computation.27 | async-start | bytes 4718592 | tf_op jit(solution)/shard_map/reduce_scatter | solution.py:261
  496.4 13.0 %copy-start.5 = (f32[128,1024]{1,0:T(8,128)S(1)}, f32[128,1024]{1,0:T(8,128)}, u32[]{:S(2)}) copy-start(f32[128,1024]{1,0:T(8,128)} %param.21) | copy-start | bytes 1572868
  496.4 13.0 %copy-start.65 = (f32[1,1024]{1,0:T(1,128)S(1)}, f32[1,1024]{1,0:T(1,128)}, u32[]{:S(2)}) copy-start(f32[1,1024]{1,0:T(1,128)} %copy-done.64) | copy-start | bytes 12292
  496.5 15.8 %copy-start.45 = (bf16[512,1024]{1,0:T(8,128)(2,1)S(1)}, bf16[512,1024]{1,0:T(8,128)(2,1)}, u32[]{:S(2)}) copy-start(bf16[512,1024]{1,0:T(8,128)(2,1)} %all-gather.8.cloned.1.call-done) | copy-start | bytes 3145732
  496.5 159.9 %reduce-scatter.24.cloned.1.call-start = ((), (), s32[]{:S(2)}) async-start(), calls=%async_computation.23 | async-start | bytes 1179648 | tf_op jit(solution)/shard_map/reduce_scatter | solution.py:318
  499.1 194.3 %reduce-scatter.34.cloned.1.call-start = ((), (), s32[]{:S(2)}) async-start(), calls=%async_computation.28 | async-start | bytes 589824
  512.2 226.1 %reduce-scatter.22.cloned.1.call-start = ((), (), s32[]{:S(2)}) async-start(), calls=%async_computation.22 | async-start | bytes 2359296 | tf_op jit(solution)/shard_map/reduce_scatter | solution.py:317
  514.3 298.6 %reduce-scatter.26.cloned.1.call-start = ((), (), s32[]{:S(2)}) async-start(), calls=%async_computation.24 | async-start | bytes 9437184 | tf_op jit(solution)/shard_map/reduce_scatter | solution.py:260
  523.0 364.5 %reduce-scatter.28.cloned.1.call-start = ((), (), s32[]{:S(2)}) async-start(), calls=%async_computation.25 | async-start | bytes 9437184 | tf_op jit(solution)/shard_map/reduce_scatter | solution.py:260
  540.9 77.0 %copy-start.19 = (f32[16,128,128]{2,1,0:T(8,128)S(1)}, f32[16,128,128]{2,1,0:T(8,128)}, u32[]{:S(2)}) copy-start(f32[16,128,128]{2,1,0:T(8,128)} %param.29) | copy-start | bytes 3145732
  622.0 40.0 %copy-start.40 = (f32[128,1024]{1,0:T(8,128)S(1)}, f32[128,1024]{1,0:T(8,128)}, u32[]{:S(2)}) copy-start(f32[128,1024]{1,0:T(8,128)} %get-tuple-element.179) | copy-start | bytes 1572868
  622.0 40.0 %copy-start.47 = (bf16[128,1024]{1,0:T(8,128)(2,1)S(1)}, bf16[128,1024]{1,0:T(8,128)(2,1)}, u32[]{:S(2)}) copy-start(bf16[128,1024]{1,0:T(8,128)(2,1)} %reduce-scatter.20.cloned.1.call-done) | copy-start | bytes 786436
  622.0 84.3 %copy-start.76 = (f32[2,128]{1,0:T(2,128)S(1)}, f32[2,128]{1,0:T(2,128)}, u32[]{:S(2)}) copy-start(f32[2,128]{1,0:T(2,128)} %param.25) | copy-start | bytes 3076
  622.0 84.3 %copy-start.77 = (f32[2,128]{1,0:T(2,128)S(1)}, f32[2,128]{1,0:T(2,128)}, u32[]{:S(2)}) copy-start(f32[2,128]{1,0:T(2,128)} %param.30) | copy-start | bytes 3076
  622.0 116.3 %copy-start.28 = (f32[4,128,128]{1,2,0:T(8,128)S(1)}, f32[4,128,128]{1,2,0:T(8,128)}, u32[]{:S(2)}) copy-start(f32[4,128,128]{1,2,0:T(8,128)} %copy-done.27) | copy-start | bytes 786436
  656.4 49.9 %copy-start.78 = (f32[2,128]{1,0:T(2,128)S(1)}, f32[2,128]{1,0:T(2,128)}, u32[]{:S(2)}) copy-start(f32[2,128]{1,0:T(2,128)} %param.31) | copy-start | bytes 3076
  706.3 107.9 %copy-start.75 = (f32[2,128]{1,0:T(2,128)}, f32[2,128]{1,0:T(2,128)S(1)}, u32[]{:S(2)}) copy-start(f32[2,128]{1,0:T(2,128)S(1)} %psum.7) | copy-start | bytes 3076
  (56 other events, 135.8 us)
Sparse Core Ops, SparseCore 0:
  21.9 28.2 all-gather.7
  52.7 22.8 all-gather.9
  86.0 43.6 reduce-scatter.13
  131.1 44.8 all-gather.17
  178.0 26.7 all-gather.11
  207.1 35.9 all-gather.13
  245.6 36.5 all-gather.15
  344.8 50.0 reduce-scatter.17
  408.9 33.7 reduce-scatter.15
  445.3 26.4 all-gather.19
  482.7 26.6 reduce-scatter.19
  512.6 49.5 reduce-scatter.29
  565.6 51.0 reduce-scatter.31
  620.4 35.9 reduce-scatter.23
  659.3 34.0 reduce-scatter.33
  697.1 41.0 reduce-scatter.21
  741.6 71.2 reduce-scatter.25
  816.2 71.2 reduce-scatter.27
